TPU v7x, 256 devices: a whole 4x4x8 slice. The times are simulated.
256 devices in a mesh: dp: 64 (over y, z, core), tensor: 4 (over x).
Axes of the slice: x: 4, y: 4, z: 8, core: 2. Of those that a mesh axis runs over, the one named last changes fastest.
Arguments:
- activations: bfloat16 [32768, 8192], P('dp', 'tensor'), may hold values from -2000 to 2000
- norm_gain: float32 [8192], replicated, may hold values from 0.5 to 12
- w_query: bfloat16 [8192, 4096], P('dp', 'tensor'), may hold values from -0.0625 to 0.0625
- w_key: bfloat16 [8192, 512], P('dp', 'tensor'), may hold values from -0.0625 to 0.0625
- w_value: bfloat16 [8192, 512], P('dp', 'tensor'), may hold values from -0.0625 to 0.0625
- lengths: int32 [128], replicated, may hold values from 128 to 256
- languages: int32 [128], replicated, may hold values from 0 to 29
- lang_caps: int32 [30], replicated, may hold values from 128 to 256
- dest_shard: int32 [128], replicated, may hold values from 0 to 63, as said below
Outputs:
- attended: bfloat16 [32768, 4096], P('dp', 'tensor')
Inputs may be any that keep to these rules, and one draw needn't show every extreme that they name: `dest_shard`: every data shard receives exactly 2 documents.
All inputs are finite; a program needn't handle non-finite values.
Results may differ from a plain program's by a relative error of at most 0.007.
The roundings to bfloat16 on the way count: a program that leaves them out, or rounds other values in their place, can miss the bound.
Values may be sent and summed in bfloat16 or wider, within the bound.
A program may use at most 128 MiB of HBM per device.

v0:
```python
import math
import jax
import jax.numpy as jnp
from jax import lax
from jax.sharding import PartitionSpec as P

HEAD_WIDTH = 128
rope_base = 500000.0
norm_eps = 1e-05


def rotary_embedding(vectors, token_positions):
    half_width = vectors.shape[-1] // 2
    steps_range = jnp.arange(half_width, dtype=jnp.float32)
    frequency = jnp.exp(steps_range * (-2.0 * math.log(rope_base) / vectors.shape[-1]))
    angles = token_positions[..., None, None] * frequency
    cosine = jnp.cos(angles)
    sine_table = jnp.sin(angles)
    first_half = vectors[..., :half_width]
    second_half = vectors[..., half_width:]
    return jnp.concatenate(
        [
            first_half * cosine - second_half * sine_table,
            second_half * cosine + first_half * sine_table,
        ],
        axis=-1,
    )


def project(source_rows, norm_gain, w_query, w_key, w_value):
    gathered = lax.all_gather(source_rows, "tensor", axis=1, tiled=True)
    widened = gathered.astype(jnp.float32)
    row_scale = lax.rsqrt(jnp.mean(widened * widened, axis=1, keepdims=True) + norm_eps)
    normed = (widened * row_scale * norm_gain).astype(jnp.bfloat16)
    pieces = (
        lax.all_gather(w_query, "dp", axis=0, tiled=True),
        lax.all_gather(w_key, "dp", axis=0, tiled=True),
        lax.all_gather(w_value, "dp", axis=0, tiled=True),
    )
    return tuple(
        (
            jnp.dot(normed, weight_piece, preferred_element_type=jnp.float32)
            for weight_piece in pieces
        )
    )


def rotate_round(query_part, key_portion, value_portion, token_positions, head_dim):
    total_rows = query_part.shape[0]
    rotated_query = rotary_embedding(
        query_part.reshape(total_rows, -1, head_dim), token_positions
    ).reshape(total_rows, -1)
    rotated_key = rotary_embedding(
        key_portion.reshape(total_rows, -1, head_dim), token_positions
    ).reshape(total_rows, -1)
    return jnp.concatenate([rotated_query, rotated_key, value_portion], axis=1).astype(jnp.bfloat16)


def attend(packed, doc_lengths, query_width, key_width, head_dim, doc_max):
    total_rows = packed.shape[0]
    doc_total = total_rows // doc_max
    value_head_rows = key_width // head_dim
    heads_per_group = query_width // key_width
    queries = packed[:, :query_width].reshape(
        doc_total, doc_max, value_head_rows, heads_per_group, head_dim
    )
    key_rows = packed[:, query_width : query_width + key_width].reshape(
        doc_total, doc_max, value_head_rows, head_dim
    )
    value_rows = packed[:, query_width + key_width :].reshape(
        doc_total, doc_max, value_head_rows, head_dim
    )
    scores = jnp.einsum(
        "jqhgd,jkhd->jhgqk", queries, key_rows, preferred_element_type=jnp.float32
    ) / math.sqrt(head_dim)
    order_range = jnp.arange(doc_max)
    causal = order_range[:, None] >= order_range[None, :]
    scores = jnp.where(causal, scores, -jnp.inf)
    row_peak = jnp.max(scores, axis=-1, keepdims=True)
    exponent = jnp.exp(scores - row_peak)
    probability = (exponent / jnp.sum(exponent, axis=-1, keepdims=True)).astype(jnp.bfloat16)
    blended = jnp.einsum(
        "jhgqk,jkhd->jqhgd", probability, value_rows, preferred_element_type=jnp.float32
    )
    blended = blended.reshape(doc_total, doc_max, query_width)
    row_valid = order_range[None, :] < doc_lengths[:, None]
    result = jnp.where(row_valid[..., None], blended, 0.0)
    return result.reshape(total_rows, query_width).astype(jnp.bfloat16)


def local(
    activations, norm_gain, w_query, w_key, w_value, lengths, languages, lang_caps, dest_shard
):
    shard_count = lax.axis_size("dp")
    my_shard = lax.axis_index("dp")
    doc_count = lengths.shape[0]
    token_rows = activations.shape[0]
    rows_peer = token_rows // doc_count
    doc_max = rows_peer * shard_count
    docs_here = doc_count // shard_count
    head_dim = HEAD_WIDTH
    query_width = w_query.shape[1]
    key_width = w_key.shape[1]
    language_table = jnp.arange(lang_caps.shape[0])
    cap_of_doc = jnp.sum(
        jnp.where(languages[:, None] == language_table[None, :], lang_caps[None, :], 0), axis=1
    )
    capped = jnp.minimum(lengths, cap_of_doc)
    doc_order = jnp.arange(doc_count)
    same_dest = dest_shard[:, None] == dest_shard[None, :]
    doc_rank = jnp.sum(
        (same_dest & (doc_order[None, :] < doc_order[:, None])).astype(jnp.int32), axis=1
    )
    target_slot = dest_shard * docs_here + doc_rank
    holder = jnp.sum(
        jnp.where(doc_order[:, None] == target_slot[None, :], doc_order[None, :], 0), axis=1
    )
    mine = lax.dynamic_slice_in_dim(holder, my_shard * docs_here, docs_here)
    doc_lengths = jnp.take(capped, mine)
    holder_grid = jnp.transpose(holder.reshape(shard_count, docs_here))
    send_index = (
        holder_grid[:, None, :] * rows_peer + jnp.arange(rows_peer)[None, :, None]
    ).reshape(-1)
    outgoing = jnp.take(activations, send_index, axis=0).reshape(
        docs_here, rows_peer, shard_count, -1
    )
    arrived = lax.all_to_all(outgoing, "dp", split_axis=2, concat_axis=2, tiled=True)
    moved_rows = arrived.reshape(docs_here * doc_max, -1)
    query_part, key_portion, value_portion = project(moved_rows, norm_gain, w_query, w_key, w_value)
    token_positions = jnp.tile(jnp.arange(doc_max), docs_here).astype(jnp.float32)
    packed = rotate_round(query_part, key_portion, value_portion, token_positions, head_dim)
    return attend(packed, doc_lengths, query_width, key_width, head_dim, doc_max)


def solution(mesh):
    return jax.shard_map(
        local,
        mesh=mesh,
        in_specs=(
            P("dp", "tensor"),
            P(),
            P("dp", "tensor"),
            P("dp", "tensor"),
            P("dp", "tensor"),
            P(),
            P(),
            P(),
            P(),
        ),
        out_specs=P("dp", "tensor"),
        check_vma=False,
    )
```

profile of v0, /device:TPU:1, one launch (start us, length us, event | category | flops | bytes accessed | tf_op | source)
XLA Modules:
  0.0 453.7 jit_solution(18384676850716704676)
XLA Ops:
  6.5 0.0 copy-start
  6.5 0.0 all-gather.5.cloned.1.call-start
  6.5 1.0 convert_reduce_fusion
  7.5 0.7 multiply_add_fusion
  8.2 0.1 select_reduce_fusion
  8.3 0.1 mul.188
  8.5 0.1 copy.35
  8.6 0.1 add.84
  8.7 0.1 copy.36
  8.8 0.0 copy-done
  8.8 3.3 gather_fusion.1
  12.2 3.8 copy_select_fusion
  16.0 64.1 %all_to_all.5 = bf16[2,4,64,2048]{3,1,0,2:T(4,128)(2,1)S(1)} all-to-all(bf16[2,4,64,2048]{3,1,0,2:T(4,128)(2,1)S(1)} %copy_select_fusion), channel_id=1, replica_groups=mesh['dp'=64,'tensor'=4] {'dp'}, dimensions={2} | all-to-all | bytes 4194304 | tf_op jit(solution)/shard_map/all_to_all | solution.py:127
  80.1 2.5 copy.38
  82.7 0.0 all-gather.5.cloned.1.call-update
  82.7 0.0 all-gather.9.cloned.1.call-start
  82.7 0.7 all-gather.9.cloned.1.call-update
  83.4 0.0 all-gather.7.cloned.1.call-start
  83.5 0.7 all-gather.7.cloned.1.call-update
  84.2 0.0 all-gather.11.cloned.1.call-start
  84.2 0.5 all-gather.11.cloned.1.call-update
  84.8 0.0 copy-done.2
  84.8 0.0 copy-done.3
  84.8 0.1 select_reduce_fusion.1
  84.9 0.1 compare_select_fusion.2
  85.0 0.6 gather_fusion
  85.6 0.1 and_select_fusion
  85.7 0.1 iota_compare_fusion.4
  85.8 1.0 multiply_cosine_fusion
  86.8 0.0 copy-start.1
  86.8 77.9 %all-gather.5.cloned.1.call-done = bf16[512,8192]{1,0:T(8,128)(2,1)} async-done(((bf16[512,2048]{1,0:T(8,128)(2,1)}), bf16[512,8192]{1,0:T(8,128)(2,1)}) %all-gather.5.cloned.1.call-update) | async-done | bytes 8388624 | tf_op jit(solution)/shard_map/all_gather | solution.py:31
  164.7 5.1 %fusion = f32[512]{0:T(512)S(1)} fusion(bf16[512,8192]{1,0:T(8,128)(2,1)} %all-gather.5.cloned.1.call-done), kind=kLoop, calls=%fused_computation.4 | loop fusion | flops 12582400 | bytes 8390656 | tf_op jit(solution)/shard_map/reduce_sum | solution.py:33
  169.8 76.8 %all-gather.9.cloned.1.call-done = bf16[8192,128]{1,0:T(8,128)(2,1)} async-done(((bf16[128,128]{1,0:T(8,128)(2,1)}), bf16[8192,128]{1,0:T(8,128)(2,1)}) %all-gather.9.cloned.1.call-update) | async-done | bytes 2097168 | tf_op jit(solution)/shard_map/all_gather | solution.py:37
  246.6 6.5 %convolution_bitcast_fusion.1 = f32[512,1,128]{0,2,1:T(8,128)S(1)} fusion(bf16[8192,128]{1,0:T(8,128)(2,1)} %all-gather.9.cloned.1.call-done, bf16[512,8192]{1,0:T(8,128)(2,1)} %all-gather.5.cloned.1.call-done, f32[8192]{0:T(1024)S(1)} %copy-done.1, f32[512]{0:T(512)S(1)} %add_rsqrt_fusion), kind=kOutput, calls=%fused_computation.22 | convolution fusion | flops 1090519040 | bytes 10782720 | tf_op jit(solution)/shard_map/dot_general | solution.py:42
  253.1 0.6 fusion.19
  253.7 0.1 copy.49
  253.8 70.6 %all-gather.7.cloned.1.call-done = bf16[8192,128]{1,0:T(8,128)(2,1)} async-done(((bf16[128,128]{1,0:T(8,128)(2,1)}), bf16[8192,128]{1,0:T(8,128)(2,1)}) %all-gather.7.cloned.1.call-update) | async-done | bytes 2097168 | tf_op jit(solution)/shard_map/all_gather | solution.py:38
  324.4 6.4 %convolution_convert_fusion = bf16[512,128]{1,0:T(8,128)(2,1)S(1)} fusion(bf16[8192,128]{1,0:T(8,128)(2,1)} %all-gather.7.cloned.1.call-done, bf16[512,8192]{1,0:T(8,128)(2,1)} %all-gather.5.cloned.1.call-done, f32[8192]{0:T(1024)S(1)} %copy-done.1, f32[512]{0:T(512)S(1)} %add_rsqrt_fusion), kind=kOutput, calls=%fused_computation.23 | convolution fusion | flops 1090584576 | bytes 10651648 | tf_op jit(solution)/shard_map/dot_general | solution.py:42
  330.8 93.0 %all-gather.11.cloned.1.call-done = bf16[8192,1024]{1,0:T(8,128)(2,1)} async-done(((bf16[128,1024]{1,0:T(8,128)(2,1)}), bf16[8192,1024]{1,0:T(8,128)(2,1)}) %all-gather.11.cloned.1.call-update) | async-done | bytes 16777232 | tf_op jit(solution)/shard_map/all_gather | solution.py:36
  423.8 14.5 %convolution_bitcast_fusion = f32[64,8,8,128]{3,1,2,0:T(8,128)S(1)} fusion(bf16[8192,1024]{1,0:T(8,128)(2,1)} %all-gather.11.cloned.1.call-done, bf16[512,8192]{1,0:T(8,128)(2,1)} %all-gather.5.cloned.1.call-done, f32[8192]{0:T(1024)S(1)} %copy-done.1, f32[512]{0:T(512)S(1)} %add_rsqrt_fusion), kind=kOutput, calls=%fused_computation.21 | convolution fusion | flops 8606711808 | bytes 27297792 | tf_op jit(solution)/shard_map/dot_general | solution.py:42
  438.3 0.5 copy.51
  438.8 0.9 subtract_convert_fusion
  439.7 0.6 pad_maximum_fusion
  440.3 0.8 fusion.4
  441.0 0.9 fusion.3
  441.9 2.3 fusion.9
  444.2 1.7 copy.43
  445.9 1.2 fusion.5
  (19 shorter events, 0.2 us)
Async XLA Ops:
  6.5 2.3 copy-start
  6.5 158.2 %all-gather.5.cloned.1.call-start = ((), (), s32[]{:S(2)}) async-start(), calls=%async_computation.1 | async-start | bytes 10485760 | tf_op jit(solution)/shard_map/all_gather | solution.py:31
  80.1 4.6 %copy-start.2 = (s32[30]{0:T(128)S(1)}, s32[30]{0:T(128)}, u32[]{:S(2)}) copy-start(s32[30]{0:T(128)} %param.16) | copy-start | bytes 364
  80.1 4.6 %copy-start.3 = (s32[128]{0:T(128)S(1)}, s32[128]{0:T(128)}, u32[]{:S(2)}) copy-start(s32[128]{0:T(128)} %param.15) | copy-start | bytes 1540
  80.1 4.7 %copy-start.4 = (s32[128]{0:T(128)S(1)}, s32[128]{0:T(128)}, u32[]{:S(2)}) copy-start(s32[128]{0:T(128)} %param.14) | copy-start | bytes 1540
  82.7 164.0 %all-gather.9.cloned.1.call-start = ((), (), s32[]{:S(2)}) async-start(), calls=%async_computation.3 | async-start | bytes 2129920 | tf_op jit(solution)/shard_map/all_gather | solution.py:37
  83.4 241.0 %all-gather.7.cloned.1.call-start = ((), (), s32[]{:S(2)}) async-start(), calls=%async_computation.2 | async-start | bytes 2129920 | tf_op jit(solution)/shard_map/all_gather | solution.py:38
  84.2 339.6 %all-gather.11.cloned.1.call-start = ((), (), s32[]{:S(2)}) async-start(), calls=%async_computation.4 | async-start | bytes 17039360 | tf_op jit(solution)/shard_map/all_gather | solution.py:36
  86.8 159.8 %copy-start.1 = (f32[8192]{0:T(1024)S(1)}, f32[8192]{0:T(1024)}, u32[]{:S(2)}) copy-start(f32[8192]{0:T(1024)} %param.10) | copy-start | bytes 98308
Sparse Core Ops, SparseCore 0:
  82.8 81.8 all-gather.4
  167.5 79.0 all-gather.8
  249.4 74.9 all-gather.6
  327.1 96.6 all-gather.10
where the time goes:
time: 454 us
  waiting for transfers between devices  320 us (70%)
  blocking collectives  64.1 us (14%)
  matrix products  30.4 us (7%)
  other arithmetic  16.2 us (4%)
  between operations  13.3 us (3%)
  local copies, waits for them, and re-layouts  9.25 us (2%)
    all_gather x1, waiting for transfers between devices, project(): lax.all_gather(w_query, 'dp', axis=0, tiled=True)  93 us
    all_gather x1, waiting for transfers between devices, project(): gathered = lax.all_gather(source_rows, 'tensor', axis=1, tiled=True)  77.9 us
    all_gather x1, waiting for transfers between devices, project(): lax.all_gather(w_key, 'dp', axis=0, tiled=True)  76.8 us
    all_gather x1, waiting for transfers between devices, project(): lax.all_gather(w_value, 'dp', axis=0, tiled=True)  70.6 us
    all_to_all x1, blocking collectives, local(): lax.all_to_all(outgoing, 'dp', split_axis=2, concat_axis=2, tiled=True)  64.1 us
    dot_general x3, matrix products, project(): jnp.dot(normed, weight_piece, preferred_element_type=jnp.float32)  27.4 us
  transfers between devices with their start and end apart: 4, of which 4 were waited for; matrix products, arithmetic and copies ran while one was open for 5% of the time, Pallas kernels for 0%

commit v1 on v0

--- a/solution.py
+++ b/solution.py
@@ -7,6 +7,28 @@
 HEAD_WIDTH = 128
 rope_base = 500000.0
 norm_eps = 1e-05
+
+
+def laid_out(blocks, dim):
+    blocks = jnp.moveaxis(blocks, 0, dim)
+    lengths = blocks.shape
+    return blocks.reshape(*lengths[:dim], lengths[dim] * lengths[dim + 1], *lengths[dim + 2 :])
+
+
+def gather_around(value, axis, dim):
+    size = lax.axis_size(axis)
+    pairs = [(i, (i + 1) % size) for i in range(size)]
+    back = [(b, a) for a, b in pairs]
+    lower, upper = ([], [])
+    for step in range(size - 1):
+        if step % 2 == 0:
+            lower.append(lax.ppermute(lower[-1] if lower else value, axis, pairs))
+        else:
+            upper.append(lax.ppermute(upper[-1] if upper else value, axis, back))
+    tiles = jnp.stack([*lower[::-1], value, *upper])
+    shift = lax.axis_index(axis) - len(lower)
+    tiles = tiles[(jnp.arange(size) - shift) % size]
+    return laid_out(tiles, dim)
 
 
 def rotary_embedding(vectors, token_positions):
@@ -28,7 +50,7 @@
 
 
 def project(source_rows, norm_gain, w_query, w_key, w_value):
-    gathered = lax.all_gather(source_rows, "tensor", axis=1, tiled=True)
+    gathered = gather_around(source_rows, "tensor", 1)
     widened = gathered.astype(jnp.float32)
     row_scale = lax.rsqrt(jnp.mean(widened * widened, axis=1, keepdims=True) + norm_eps)
     normed = (widened * row_scale * norm_gain).astype(jnp.bfloat16)

time: 454 us -> 330 us (0.73)
  waiting for transfers between devices: 320 us -> 93.3 us
  local copies, waits for them, and re-layouts: 9.25 us -> 71.9 us
  other arithmetic: 16.2 us -> 48.1 us
    all_gather x1, waiting for transfers between devices: 93 us -> 0.02 us  [project(): lax.all_gather(w_query, 'dp', axis=0, tiled=True)]
    ppermute x0 -> x3, waiting for transfers between devices: none -> 91.1 us  [the longest x2 91.1 us: gather_around(): lower.append(lax.ppermute(lower[-1] if lower else value, axis, pairs))]
    all_gather x1 -> x0, waiting for transfers between devices: 77.9 us -> none  [project(): gathered = lax.all_gather(source_rows, 'tensor', axis=1, tiled=True)]
    all_gather x1, waiting for transfers between devices: 76.8 us -> 0.01 us  [project(): lax.all_gather(w_key, 'dp', axis=0, tiled=True)]
    all_gather x1, waiting for transfers between devices: 70.6 us -> 0.01 us  [project(): lax.all_gather(w_value, 'dp', axis=0, tiled=True)]
    dot_general x0 -> x1, local copies, waits for them, and re-layouts: none -> 21.3 us  [project(): jnp.dot(normed, weight_piece, preferred_element_type=jnp.float32)]
    convert_element_type x0 -> x2, other arithmetic: none -> 20.8 us  [the longest x1 11.3 us: project(): widened = gathered.astype(jnp.float32)]
    convert_element_type x0 -> x1, local copies, waits for them, and re-layouts: none -> 16.4 us  [project(): widened = gathered.astype(jnp.float32)]
  transfers between devices with their start and end apart: 4 -> 6, of which waited for: 4 -> 2; matrix products, arithmetic and copies ran while one was open for 5% -> 33% of each run, Pallas kernels for 0% -> 0%
where the time goes in v1:
time: 330 us; the launch traced here: 327 us
  waiting for transfers between devices  93.3 us (28%)
  local copies, waits for them, and re-layouts  71.9 us (22%)
  blocking collectives  68.2 us (21%)
  other arithmetic  48.1 us (15%)
  matrix products  29.4 us (9%)
  between operations  13.4 us (4%)
    ppermute x2, waiting for transfers between devices, gather_around(): lower.append(lax.ppermute(lower[-1] if lower else value, axis, pairs))  91.1 us
    all_to_all x1, blocking collectives, local(): lax.all_to_all(outgoing, 'dp', split_axis=2, concat_axis=2, tiled=True)  68.2 us
    dot_general x3, matrix products, project(): jnp.dot(normed, weight_piece, preferred_element_type=jnp.float32)  26.4 us
    dot_general x1, local copies, waits for them, and re-layouts, project(): jnp.dot(normed, weight_piece, preferred_element_type=jnp.float32)  21.3 us
    convert_element_type x1, local copies, waits for them, and re-layouts, project(): widened = gathered.astype(jnp.float32)  16.4 us
    gather x3, local copies, waits for them, and re-layouts, gather_around(): tiles = tiles[(jnp.arange(size) - shift) % size]  13.9 us
    mul x2, local copies, waits for them, and re-layouts, project(): normed = (widened * row_scale * norm_gain).astype(jnp.bfloat16)  11.5 us
    convert_element_type x1, other arithmetic, project(): widened = gathered.astype(jnp.float32)  11.3 us
  transfers between devices with their start and end apart: 6, of which 2 were waited for; matrix products, arithmetic and copies ran while one was open for 33% of the time, Pallas kernels for 0%

profile of v1, /device:TPU:1, one launch (start us, length us, event | category | flops | bytes accessed | tf_op | source)
XLA Modules:
  0.0 327.0 jit_solution(1093485672830293112)
XLA Ops:
  6.5 0.7 all-gather.6.cloned.1.call-update
  7.3 0.7 all-gather.4.cloned.1.call-update
  8.1 0.7 all-gather.8.cloned.1.call-update
  8.7 0.9 convert_reduce_fusion
  9.6 0.7 multiply_add_fusion
  10.3 0.1 select_reduce_fusion
  10.4 0.1 mul.206
  10.6 0.1 copy.59
  10.7 0.1 add.108
  10.8 0.1 copy.60
  11.0 3.3 %gather_fusion.1 = bf16[512,2048]{1,0:T(8,128)(2,1)} fusion(bf16[512,2048]{1,0:T(8,128)(2,1)S(1)} %copy-done, s32[1024]{0:T(1024)S(1)} %pad_clamp_fusion.1), kind=kCustom, calls=%fused_computation.1 | custom fusion | bytes 4196352 | tf_op jit(solution)/shard_map/jit(_take)/gather | solution.py:146
  14.3 3.8 %copy_select_fusion = bf16[2,4,64,2048]{3,1,0,2:T(4,128)(2,1)S(1)} fusion(bf16[2,4,64,2048]{3,2,1,0:T(8,128)(2,1)} %bitcast.87, pred[2,4,64]{1,0,2:T(4,128)(4,1)S(1)} %copy.60), kind=kLoop, calls=%fused_computation.25 | loop fusion | flops 1048576 | bytes 4194816 | tf_op jit(solution)/shard_map/jit(_take)/select_n | solution.py:146
  18.2 68.2 %all_to_all.5 = bf16[2,4,64,2048]{3,1,0,2:T(4,128)(2,1)S(1)} all-to-all(bf16[2,4,64,2048]{3,1,0,2:T(4,128)(2,1)S(1)} %copy_select_fusion), channel_id=1, replica_groups=mesh['dp'=64,'tensor'=4] {'dp'}, dimensions={2} | all-to-all | bytes 4194304 | tf_op jit(solution)/shard_map/all_to_all | solution.py:149
  86.4 2.5 copy.62
  88.9 1.3 collective-permute-start
  90.1 1.4 collective-permute-start.2
  91.5 45.6 %collective-permute-done = bf16[512,2048]{1,0:T(8,128)(2,1)} collective-permute-done((bf16[512,2048]{1,0:T(8,128)(2,1)}, bf16[512,2048]{1,0:T(8,128)(2,1)}, u32[]{:S(2)}, u32[]{:S(2)}) %collective-permute-start) | collective-permute-done | bytes 2097184 | tf_op jit(solution)/shard_map/ppermute | solution.py:25
  137.1 0.1 collective-permute-start.1
  137.3 0.1 select_reduce_fusion.1
  137.4 0.1 compare_select_fusion.3
  137.5 0.6 gather_fusion
  138.1 0.1 and_select_fusion.1
  138.2 0.1 iota_compare_fusion.4
  138.4 0.5 multiply_cosine_fusion
  138.9 45.6 %collective-permute-done.1 = bf16[512,2048]{1,0:T(8,128)(2,1)} collective-permute-done((bf16[512,2048]{1,0:T(8,128)(2,1)}, bf16[512,2048]{1,0:T(8,128)(2,1)}, u32[]{:S(2)}, u32[]{:S(2)}) %collective-permute-start.1) | collective-permute-done | bytes 2097184 | tf_op jit(solution)/shard_map/ppermute | solution.py:25
  184.5 4.5 %pad_maximum_fusion = bf16[4,512,2048]{2,1,0:T(8,128)(2,1)S(1)} fusion(bf16[1,512,2048]{2,1,0:T(8,128)(2,1)} %bitcast.7, bf16[1,512,2048]{2,1,0:T(8,128)(2,1)} %bitcast.6, bf16[1,512,2048]{2,1,0:T(8,128)(2,1)} %bitcast.5, bf16[1,512,2048]{2,1,0:T(8,128)(2,1)} %bitcast.4), kind=kLoop, calls=%fused_computation.14 | loop fusion | flops 12582912 | bytes 16777216 | tf_op jit(solution)/shard_map/stack | solution.py:28
  189.0 3.8 %fusion.31 = (bf16[4,512,1024]{2,1,0:T(8,128)(2,1)}, bf16[4,512,1024]{2,1,0:T(8,128)(2,1)}) fusion(bf16[4,512,2048]{2,1,0:T(8,128)(2,1)S(1)} %pad_maximum_fusion), kind=kLoop, calls=%fused_computation.80 | loop fusion | bytes 16777216 | tf_op jit(solution)/shard_map/gather | solution.py:30
  192.8 5.0 %gather_fusion.3 = bf16[4,512,1024]{2,1,0:T(8,128)(2,1)} fusion(bf16[4,512,1024]{2,1,0:T(8,128)(2,1)} %get-tuple-element.6, s32[1024]{0:T(1024)S(1)} %pad_clamp_fusion), kind=kCustom, calls=%fused_computation.3 | custom fusion | bytes 8388624 | tf_op jit(solution)/shard_map/gather | solution.py:30
  197.9 5.0 %gather_fusion.2 = bf16[4,512,1024]{2,1,0:T(8,128)(2,1)} fusion(bf16[4,512,1024]{2,1,0:T(8,128)(2,1)} %get-tuple-element.5, s32[1024]{0:T(1024)S(1)} %pad_clamp_fusion), kind=kCustom, calls=%fused_computation.2 | custom fusion | bytes 8388624 | tf_op jit(solution)/shard_map/gather | solution.py:30
  202.9 11.3 %convert_bitcast_fusion = f32[512,4,2048]{2,0,1:T(8,128)} fusion(bf16[4,512,1024]{2,1,0:T(8,128)(2,1)} %gather_fusion.3, bf16[4,512,1024]{2,1,0:T(8,128)(2,1)} %gather_fusion.2), kind=kLoop, calls=%fused_computation.6 | loop fusion | flops 16777216 | bytes 25165824 | tf_op jit(solution)/shard_map/convert_element_type | solution.py:54
  214.2 16.4 %copy.64 = f32[512,4,2048]{0,2,1:T(8,128)} copy(f32[512,4,2048]{2,0,1:T(8,128)} %convert_bitcast_fusion) | data formatting | bytes 33554432 | tf_op jit(solution)/shard_map/convert_element_type | solution.py:54
  230.6 5.1 %fusion = f32[512]{0:T(512)S(1)} fusion(bf16[4,512,1024]{2,1,0:T(8,128)(2,1)} %gather_fusion.3, bf16[4,512,1024]{2,1,0:T(8,128)(2,1)} %gather_fusion.2), kind=kLoop, calls=%fused_computation.7 | loop fusion | flops 25165312 | bytes 8390656 | tf_op jit(solution)/shard_map/reduce_sum | solution.py:55
  235.7 9.5 %fusion.4 = bf16[512,8192]{0,1:T(8,128)(2,1)} fusion(f32[512,4,2048]{0,2,1:T(8,128)} %copy.64, f32[8192]{0:T(1024)S(1)} %copy-done.2, f32[512]{0:T(512)S(1)} %add_rsqrt_fusion), kind=kLoop, calls=%fused_computation.12 | loop fusion | flops 12582912 | bytes 25200640 | tf_op jit(solution)/shard_map/convert_element_type | solution.py:56
  245.3 5.8 %convolution_bitcast_fusion = f32[512,1,128]{0,2,1:T(8,128)S(1)} fusion(bf16[512,8192]{0,1:T(8,128)(2,1)} %fusion.4, bf16[8192,128]{1,0:T(8,128)(2,1)} %all-gather.6.cloned.1.call-done), kind=kOutput, calls=%fused_computation.28 | convolution fusion | flops 1073741824 | bytes 10747904 | tf_op jit(solution)/shard_map/dot_general | solution.py:64
  251.0 0.6 fusion.23
  251.6 0.1 copy.79
  251.7 8.1 %fusion.5 = bf16[512,4,2048]{2,0,1:T(8,128)(2,1)} fusion(f32[4,2048]{1,0:T(4,128)S(1)} %mul.223, f32[512]{0:T(512)S(1)} %add_rsqrt_fusion, bf16[4,512,1024]{2,1,0:T(8,128)(2,1)} %gather_fusion.3, bf16[4,512,1024]{2,1,0:T(8,128)(2,1)} %gather_fusion.2), kind=kLoop, calls=%fused_computation.13 | loop fusion | flops 29360128 | bytes 16812032 | tf_op jit(solution)/shard_map/mul | solution.py:56
  259.8 11.5 %copy.65 = bf16[512,4,2048]{0,2,1:T(8,128)(2,1)} copy(bf16[512,4,2048]{2,0,1:T(8,128)(2,1)} %fusion.5) | data formatting | bytes 16777216 | tf_op jit(solution)/shard_map/mul | solution.py:56
  271.4 6.4 %convolution_convert_fusion = bf16[512,128]{1,0:T(8,128)(2,1)S(1)} fusion(bf16[512,8192]{0,1:T(8,128)(2,1)} %fusion.4, bf16[8192,128]{1,0:T(8,128)(2,1)} %all-gather.4.cloned.1.call-done), kind=kOutput, calls=%fused_computation.29 | convolution fusion | flops 1073807360 | bytes 10616832 | tf_op jit(solution)/shard_map/dot_general | solution.py:64
  277.8 21.3 %copy.66 = bf16[1024,8192]{1,0:T(8,128)(2,1)} copy(bf16[1024,8192]{0,1:T(8,128)(2,1)} %bitcast.85) | data formatting | bytes 33554432 | tf_op jit(solution)/shard_map/dot_general | solution.py:64
  299.0 14.2 %fusion.32 = f32[512,8,128]{0,2,1:T(8,128)S(1)} fusion(bf16[512,8192,1]{0,1,2:T(8,128)(2,1)} %bitcast.88, bf16[8,128,8192]{2,1,0:T(8,128)(2,1)} %bitcast.86), kind=kOutput, calls=%fused_computation.81 | convolution fusion | flops 8589934592 | bytes 27262976 | tf_op jit(solution)/shard_map/dot_general | solution.py:64
  313.3 0.3 subtract_convert_fusion
  313.6 0.1 pad_maximum_fusion.2
  313.7 0.7 fusion.7
  314.4 0.9 fusion.6
  315.3 2.3 fusion.12
  317.6 1.7 copy.72
  319.3 1.2 fusion.8
  (36 shorter events, 0.3 us)
Async XLA Ops:
  6.5 4.4 %copy-start = (bf16[512,2048]{1,0:T(8,128)(2,1)S(1)}, bf16[512,2048]{1,0:T(8,128)(2,1)}, u32[]{:S(2)}) copy-start(bf16[512,2048]{1,0:T(8,128)(2,1)} %param.9) | copy-start | bytes 6291460
  6.5 238.7 %all-gather.6.cloned.1.call-start = ((), (), s32[]{:S(2)}) async-start(), calls=%async_computation.2 | async-start | bytes 2129920 | tf_op jit(solution)/shard_map/all_gather | solution.py:59
  7.3 264.1 %all-gather.4.cloned.1.call-start = ((), (), s32[]{:S(2)}) async-start(), calls=%async_computation.1 | async-start | bytes 2129920 | tf_op jit(solution)/shard_map/all_gather | solution.py:60
  8.0 269.7 %all-gather.8.cloned.1.call-start = ((), (), s32[]{:S(2)}) async-start(), calls=%async_computation.3 | async-start | bytes 17039360 | tf_op jit(solution)/shard_map/all_gather | solution.py:58
  18.1 119.1 %copy-start.2 = (f32[8192]{0:T(1024)S(1)}, f32[8192]{0:T(1024)}, u32[]{:S(2)}) copy-start(f32[8192]{0:T(1024)} %param.10) | copy-start | bytes 98308
  18.1 119.1 %copy-start.3 = (s32[30]{0:T(128)S(1)}, s32[30]{0:T(128)}, u32[]{:S(2)}) copy-start(s32[30]{0:T(128)} %param.16) | copy-start | bytes 364
  18.1 119.1 %copy-start.4 = (s32[128]{0:T(128)S(1)}, s32[128]{0:T(128)}, u32[]{:S(2)}) copy-start(s32[128]{0:T(128)} %param.15) | copy-start | bytes 1540
  18.2 119.2 %copy-start.5 = (s32[128]{0:T(128)S(1)}, s32[128]{0:T(128)}, u32[]{:S(2)}) copy-start(s32[128]{0:T(128)} %param.14) | copy-start | bytes 1540
  88.9 48.2 %collective-permute-start = (bf16[512,2048]{1,0:T(8,128)(2,1)}, bf16[512,2048]{1,0:T(8,128)(2,1)}, u32[]{:S(2)}, u32[]{:S(2)}) collective-permute-start(bf16[512,2048]{1,0:T(8,128)(2,1)} %bitcast.3), channel_id=1, source_target_pairs={{0,1},{1,2},{2,3},{3,0},{4,5},{5,6},{6,7},{7,4},{8,9},{9,10},{10,1... | collective-permute-start | bytes 6291464 | tf_op jit(solution)/shard_map/ppermute | solution.py:25
  90.1 48.8 %collective-permute-start.2 = (bf16[512,2048]{1,0:T(8,128)(2,1)}, bf16[512,2048]{1,0:T(8,128)(2,1)}, u32[]{:S(2)}, u32[]{:S(2)}) collective-permute-start(bf16[512,2048]{1,0:T(8,128)(2,1)} %bitcast.3), channel_id=1, source_target_pairs={{1,0},{2,1},{3,2},{0,3},{5,4},{6,5},{7,6},{4,7},{9,8},{10,9},{11,1... | collective-permute-start | bytes 6291464 | tf_op jit(solution)/shard_map/ppermute | solution.py:27
  137.1 47.4 %collective-permute-start.1 = (bf16[512,2048]{1,0:T(8,128)(2,1)}, bf16[512,2048]{1,0:T(8,128)(2,1)}, u32[]{:S(2)}, u32[]{:S(2)}) collective-permute-start(bf16[512,2048]{1,0:T(8,128)(2,1)} %collective-permute-done), channel_id=1, source_target_pairs={{0,1},{1,2},{2,3},{3,0},{4,5},{5,6},{6,7},{7,4},{8,9},{9,10},{10,1... | collective-permute-start | bytes 6291464 | tf_op jit(solution)/shard_map/ppermute | solution.py:25
  315.3 5.2 %copy-start.1 = (bf16[512,2048]{1,0:T(8,128)(2,1)S(1)}, bf16[512,2048]{1,0:T(8,128)(2,1)}, u32[]{:S(2)}) copy-start(bf16[512,2048]{1,0:T(8,128)(2,1)} %param.9) | copy-start | bytes 6291460
Sparse Core Ops, SparseCore 0:
  10.1 84.4 all-gather.5
  97.3 76.1 all-gather.3
  176.3 96.6 all-gather.7
